TPU v7x, 32 devices: a whole 2x2x4 slice. The times are simulated.
32 devices in a mesh: tm: 16 (over z, y, x), space: 2 (over core).
Axes of the slice: x: 2, y: 2, z: 4, core: 2. Of those that a mesh axis runs over, the one named last changes fastest.
Arguments:
- density: float32 [16, 256, 256], P('tm', 'space'), may hold values from 0.2 to 2
- flux_x: float32 [16, 256, 256], P('tm', 'space'), may hold values from -6 to 6
- flux_y: float32 [16, 256, 256], P('tm', 'space'), may hold values from -6 to 6
Outputs:
- density_out: float32 [16, 256, 256], P('tm', 'space')
- flux_x_out: float32 [16, 256, 256], P('tm', 'space')
- flux_y_out: float32 [16, 256, 256], P('tm', 'space')
All inputs are finite; a program needn't handle non-finite values.
Results may differ from a plain program's by a relative error of at most 0.0004.
Values sent between devices are 32-bit elements; how exact they have to be, the bound alone decides.
A program may use at most 64 MiB of HBM per device.

v0:
```python
import jax
import jax.numpy as jnp
from jax import lax
from jax.sharding import PartitionSpec as P

NEWTON = 4


prox_weight = 1.0
regular_shift = 0.0001
space_weight = 0.25
flux_weight = 0.5
highest = lax.Precision.HIGHEST


def swapped(block, axis, distance):
    count = lax.axis_size(axis)
    route = []
    for low in range(count):
        high = low | 1 << distance
        if high != low and high < count:
            route += [(low, high), (high, low)]
    return lax.ppermute(block, axis, route)


def shifted(array, axis, by):
    size = lax.axis_size(axis)
    pairs = [(i, i + by) for i in range(size) if 0 <= i + by < size]
    return lax.ppermute(array, axis, pairs)


def kinetic_prox(density, flux_x, flux_y):
    square = flux_x * flux_x + flux_y * flux_y
    target = density + prox_weight + jnp.sqrt(square)
    for step in range(NEWTON):
        above = target + prox_weight
        value = (target - density) * above * above - 0.5 * prox_weight * square
        slope = above * (3.0 * target + prox_weight - 2.0 * density)
        target = target - value / slope
    shrink = target / (target + prox_weight)
    return (target, shrink * flux_x, shrink * flux_y)


def cosine_table(count):
    modes = jnp.arange(count).astype(jnp.float32)[:, None]
    points = jnp.arange(count).astype(jnp.float32)[None, :]
    table = jnp.cos(jnp.pi * modes * (2.0 * points + 1.0) / (2.0 * count))
    scales = jnp.where(modes == 0, jnp.sqrt(1.0 / count), jnp.sqrt(2.0 / count))
    return scales * table


def eigen_values(count):
    modes = jnp.arange(count).astype(jnp.float32)
    return 4.0 * jnp.sin(jnp.pi * modes / (2.0 * count)) ** 2


def move_outward(stacked, bit):
    return swapped(stacked, "tm", bit)


def move_homeward(stacked, bit):
    return swapped(stacked, "tm", bit)


def butterfly(blocks, mover):
    total = lax.axis_size("tm")
    position = lax.axis_index("tm")
    bit_count = total.bit_length() - 1
    for bit in range(bit_count):
        higher = total >> bit + 1
        lowest = 1 << bit
        shaped = blocks.reshape((higher, 2, lowest) + blocks.shape[1:])
        own_bit = position >> bit & 1
        keeping = jnp.where(own_bit == 0, shaped[:, 0], shaped[:, 1])
        leaving = jnp.where(own_bit == 0, shaped[:, 1], shaped[:, 0])
        arrived = mover(leaving, bit)
        first_half = jnp.where(own_bit == 0, keeping, arrived)
        second_half = jnp.where(own_bit == 0, arrived, keeping)
        blocks = jnp.stack([first_half, second_half], axis=1).reshape(blocks.shape)
    return blocks


def per_device(density, flux_x, flux_y):
    slabs = density.shape[0]
    rows_local = density.shape[1]
    count = density.shape[2]
    parts = lax.axis_size("space")
    modes_local = count // parts
    own_start = lax.axis_index("space") * rows_local
    mode_start = lax.axis_index("space") * modes_local
    rho, mom_x, mom_y = kinetic_prox(density, flux_x, flux_y)
    prior = shifted(rho[slabs - 1], "tm", 1)
    before = jnp.concatenate([prior[None], rho[:-1]], axis=0)
    zeroed = mom_y.at[:, :, count - 1].set(0.0)
    div_second = zeroed - jnp.concatenate(
        [jnp.zeros_like(zeroed[:, :, :1]), zeroed[:, :, :-1]], axis=2
    )
    partial_source = rho - before + flux_weight * div_second
    table = cosine_table(count)
    diff_table = jnp.concatenate(
        [table[:, :-1] - table[:, 1:], jnp.zeros_like(table[:, :1])], axis=1
    )
    stacked = jnp.concatenate([partial_source, flux_weight * mom_x], axis=1)
    column_modes = jnp.einsum("tij,kj->itk", stacked, table, precision=highest)
    left = lax.dynamic_slice(
        table, (0, own_start), (modes_local * lax.axis_size("space"), rows_local)
    )
    left_diff = lax.dynamic_slice(
        diff_table, (0, own_start), (modes_local * lax.axis_size("space"), rows_local)
    )
    both = jnp.concatenate([left, left_diff], axis=1)
    modal = lax.psum_scatter(
        jnp.einsum("ki,itj->ktj", both, column_modes, precision=highest),
        "space",
        scatter_dimension=0,
        tiled=True,
    )
    lam = eigen_values(count)
    lam_local = lax.dynamic_slice_in_dim(lam, mode_start, modes_local)
    coeff = 2.0 + regular_shift + space_weight * (lam_local[:, None] + lam[None, :])
    devices_tm = lax.axis_size("tm")
    position = lax.axis_index("tm")
    lines_local = modes_local * count
    line_group = lines_local // devices_tm
    steps_all = devices_tm * slabs
    outgoing = jnp.transpose(modal, (0, 2, 1)).reshape(devices_tm, line_group, slabs)
    incoming = butterfly(outgoing, move_outward)
    series = jnp.transpose(incoming, (1, 0, 2)).reshape(line_group, steps_all)
    line_coeff = lax.dynamic_slice_in_dim(
        coeff.reshape(lines_local), position * line_group, line_group
    )
    column = lax.broadcasted_iota(jnp.int32, (line_group, steps_all), 1)
    below_band = jnp.where(column == 0, 0.0, -1.0).astype(jnp.float32)
    above_band = jnp.where(column == steps_all - 1, 0.0, -1.0).astype(jnp.float32)
    middle_band = jnp.broadcast_to(line_coeff[:, None], (line_group, steps_all))
    solution = lax.linalg.tridiagonal_solve(
        below_band, middle_band, above_band, series[:, :, None]
    )[:, :, 0]
    blocked = solution.reshape(line_group, devices_tm, slabs)
    leading_next = jnp.concatenate(
        [solution[:, slabs::slabs], jnp.zeros((line_group, 1), jnp.float32)], axis=1
    )
    padded = jnp.concatenate([blocked, leading_next[:, :, None]], axis=2)
    returned = butterfly(jnp.transpose(padded, (1, 0, 2)), move_homeward)
    local_lines = returned.reshape(modes_local, count, slabs + 1)
    extended = jnp.transpose(local_lines, (0, 2, 1))
    phihat = extended[:, :slabs, :]
    left = lax.dynamic_slice(
        table, (mode_start, 0), (modes_local, rows_local * lax.axis_size("space"))
    )
    left_diff = lax.dynamic_slice(
        diff_table, (mode_start, 0), (modes_local, rows_local * lax.axis_size("space"))
    )
    values = jnp.einsum("ki,ktj->itj", left, extended, precision=highest)
    slopes = -jnp.einsum("ki,ktj->itj", left_diff, phihat, precision=highest)
    gathered = lax.psum_scatter(
        jnp.concatenate([values, slopes], axis=1), "space", scatter_dimension=0, tiled=True
    )
    physical = jnp.einsum("itk,kj->tij", gathered, table, precision=highest)
    potential = physical[: slabs + 1]
    grad_first = physical[slabs + 1 :]
    present = potential[:slabs]
    grad_second = jnp.concatenate(
        [present[:, :, 1:] - present[:, :, :-1], jnp.zeros_like(present[:, :, :1])], axis=2
    )
    density_out = rho - (present - potential[1:])
    flux_x_out = mom_x - flux_weight * grad_first
    flux_y_out = mom_y - flux_weight * grad_second
    return (density_out, flux_x_out, flux_y_out)


def solution(mesh):
    return jax.shard_map(
        per_device,
        mesh=mesh,
        in_specs=(P("tm", "space", None), P("tm", "space", None), P("tm", "space", None)),
        out_specs=(P("tm", "space", None), P("tm", "space", None), P("tm", "space", None)),
        check_vma=False,
    )
```

profile of v0, /device:TPU:1, one launch (start us, length us, event | category | flops | bytes accessed | tf_op | source)
XLA Modules:
  0.0 136.0 jit_solution(9983229090357020651)
XLA Ops:
  7.2 1.0 copy.72
  8.3 0.1 copy.71
  8.4 0.8 copy-done.1
  9.2 0.1 copy.74
  9.3 0.3 fusion.59
  9.6 3.9 %collective-permute-start = (f32[128,256]{0,1:T(8,128)S(1)}, f32[128,256]{0,1:T(8,128)S(1)}, u32[]{:S(2)}, u32[]{:S(2)}) collective-permute-start(f32[128,256]{0,1:T(8,128)S(1)} %bitcast.293), channel_id=1, source_target_pairs={{0,2},{2,4},{4,6},{6,8},{8,10},{10,12},{12,14},{14,16},{16,18},{18... | collective-permute-start | bytes 393224 | tf_op jit(solution)/shard_map/ppermute | solution.py:29
  13.6 0.9 cosine_multiply_fusion
  14.6 1.0 collective-permute-done
  15.7 1.5 %convolution_bitcast_fusion.2 = f32[256,256]{0,1:T(8,128)S(1)} fusion(f32[1,128,256]{1,2,0:T(8,128)S(1)} %get-tuple-element.93, f32[1,128,256]{1,2,0:T(8,128)S(1)} %get-tuple-element.92, f32[256]{0:T(256)S(1)} %multiply_add_fusion, f32[256]{0:T(256)S(1)} %convert_multiply_fusion, f32[256]{0:T(256)S(1)} %compare_select_fusion.2), kind=kOutput, calls=%fused_computation.2 | convolution fusion | flops 201588736 | bytes 527360 | tf_op jit(solution)/shard_map/tij,kj->itk/dot_general | solution.py:104
  17.2 1.3 convolution_bitcast_fusion.1
  18.6 0.2 reduce-scatter.5.cloned.1.call-start
  18.9 0.1 dynamic_slice.21
  18.9 0.1 add_bitcast_fusion
  19.1 10.8 %reduce-scatter.3.cloned.1.call-done = f32[128,1,256]{2,0,1:T(8,128)} async-done(((f32[256,1,256]{2,0,1:T(8,128)}), f32[128,1,256]{2,0,1:T(8,128)}) %reduce-scatter.3.cloned.1.call-update) | async-done | bytes 131088 | tf_op jit(solution)/shard_map/reduce_scatter | solution.py:112
  29.9 1.0 reshape_reshape_transpose.3
  30.9 0.1 fusion.55
  31.0 1.6 %collective-permute-start.1 = (f32[8,1,2048,1]{2,1,3,0:T(1,128)S(1)}, f32[8,1,2048,1]{2,1,3,0:T(1,128)S(1)}, u32[]{:S(2)}, u32[]{:S(2)}) collective-permute-start(f32[8,1,2048,1]{2,1,3,0:T(1,128)S(1)} %fusion.55), channel_id=1, source_target_pairs={{0,2},{2,0},{4,6},{6,4},{8,10},{10,8},{12,14},{14,12},{16,18},{18,... | collective-permute-start | bytes 196616 | tf_op jit(solution)/shard_map/ppermute | solution.py:23
  32.6 0.7 fusion.72
  33.3 1.3 collective-permute-done.1
  34.6 0.2 broadcast_select_fusion.2
  34.8 0.1 fusion.53
  34.9 1.6 %collective-permute-start.2 = (f32[4,2,2048,1]{2,3,1,0:T(1,128)S(1)}, f32[4,2,2048,1]{2,3,1,0:T(1,128)S(1)}, u32[]{:S(2)}, u32[]{:S(2)}) collective-permute-start(f32[4,2,2048,1]{2,3,1,0:T(1,128)S(1)} %get-tuple-element.53), channel_id=1, source_target_pairs={{0,4},{4,0},{2,6},{6,2},{8,12},{12,8},{10,14},{14,10},{16,20},{20,... | collective-permute-start | bytes 196616 | tf_op jit(solution)/shard_map/ppermute | solution.py:23
  36.5 1.7 %collective-permute-done.2 = f32[4,2,2048,1]{2,3,1,0:T(1,128)S(1)} collective-permute-done((f32[4,2,2048,1]{2,3,1,0:T(1,128)S(1)}, f32[4,2,2048,1]{2,3,1,0:T(1,128)S(1)}, u32[]{:S(2)}, u32[]{:S(2)}) %collective-permute-start.2) | collective-permute-done | bytes 65568 | tf_op jit(solution)/shard_map/ppermute | solution.py:23
  38.1 0.1 fusion.50
  38.3 0.1 pad_maximum_fusion.6
  38.5 1.5 %collective-permute-start.3 = (f32[2,4,2048,1]{2,3,1,0:T(1,128)S(1)}, f32[2,4,2048,1]{2,3,1,0:T(1,128)S(1)}, u32[]{:S(2)}, u32[]{:S(2)}) collective-permute-start(f32[2,4,2048,1]{2,3,1,0:T(1,128)S(1)} %fusion.49), channel_id=1, source_target_pairs={{0,8},{8,0},{2,10},{10,2},{4,12},{12,4},{6,14},{14,6},{16,24},{24,... | collective-permute-start | bytes 196616 | tf_op jit(solution)/shard_map/ppermute | solution.py:23
  40.0 0.7 fusion.73
  40.7 1.0 collective-permute-done.3
  41.7 0.1 fusion.46
  41.8 0.1 pad_maximum_fusion.7
  42.0 2.5 %collective-permute-start.4 = (f32[1,8,2048,1]{2,1,3,0:T(8,128)S(1)}, f32[1,8,2048,1]{2,1,3,0:T(8,128)S(1)}, u32[]{:S(2)}, u32[]{:S(2)}) collective-permute-start(f32[1,8,2048,1]{2,1,3,0:T(8,128)S(1)} %select_bitcast_fusion.3), channel_id=1, source_target_pairs={{0,16},{16,0},{2,18},{18,2},{4,20},{20,4},{6,22},{22,6},{8,24},{24... | collective-permute-start | bytes 196616 | tf_op jit(solution)/shard_map/ppermute | solution.py:23
  44.4 16.8 %broadcast_divide_fusion.1 = (f32[2048]{0:T(1024)S(1)}, f32[2048]{0:T(1024)S(1)}, f32[2048]{0:T(1024)S(1)}, f32[2048]{0:T(1024)S(1)}, f32[2048]{0:T(1024)S(1)}, /*index=5*/f32[2048]{0:T(1024)S(1)}) fusion(f32[]{:T(128)} %bitcast.75, f32[]{:T(128)} %bitcast.74, f32[]{:T(128)} %bitcast.71, f32[]{:T(128)} %bitcast.72, f32[32768]{0:T(1024)S(1)} %bitcast.313, ...), kind=kLoop, calls=%fused_computation.194 | loop fusion | flops 81920 | bytes 57456 | tf_op jit(solution)/shard_map/vmap()/eval_jaxpr/div | solution.py:136
  61.4 0.1 fusion.70
  61.5 13.0 %subtract_divide_fusion.2 = (f32[2048]{0:T(1024)S(1)}, f32[2048]{0:T(1024)S(1)}, f32[2048]{0:T(1024)S(1)}, f32[2048]{0:T(1024)S(1)}, f32[2048]{0:T(1024)S(1)}, /*index=5*/f32[2048]{0:T(1024)S(1)}, f32[2048]{0:T(1024)S(1)}) fusion(f32[2048]{0:T(1024)S(1)} %bitcast.334, f32[]{:T(128)} %bitcast.74, f32[2048]{0:T(1024)S(1)} %get-tuple-element.41, f32[]{:T(128)} %bitcast.71, ...), kind=kLoop, calls=%fused_computation.168 | loop fusion | flops 151552 | bytes 221272 | tf_op jit(solution)/shard_map/vmap()/eval_jaxpr/div | solution.py:136
  74.5 11.3 %multiply_subtract_fusion.3 = (f32[2048]{0:T(1024)S(1)}, f32[2048]{0:T(1024)S(1)}, f32[2048]{0:T(1024)S(1)}, f32[2048]{0:T(1024)S(1)}, f32[2048]{0:T(1024)S(1)},...) fusion(f32[2048]{0:T(1024)S(1)} %get-tuple-element.52, ...), kind=kLoop, calls=%fused_computation.149 | loop fusion | flops 172032 | bytes 319564 | tf_op jit(solution)/shard_map/vmap()/eval_jaxpr/sub | solution.py:136
  86.0 0.1 pad_maximum_fusion.8
  86.2 0.1 copy.89
  86.3 0.3 pad_maximum_fusion.1
  86.6 0.1 fusion.19
  86.7 1.3 collective-permute-start.5
  88.0 2.6 %collective-permute-done.5 = f32[8,1,2048,2]{2,3,0,1:T(2,128)S(1)} collective-permute-done((f32[8,1,2048,2]{2,3,0,1:T(2,128)S(1)}, f32[8,1,2048,2]{2,3,0,1:T(2,128)S(1)}, u32[]{:S(2)}, u32[]{:S(2)}) %collective-permute-start.5) | collective-permute-done | bytes 131104 | tf_op jit(solution)/shard_map/ppermute | solution.py:23
  90.6 0.1 broadcast_select_fusion.12
  90.7 0.1 fusion.20
  90.8 1.3 collective-permute-start.6
  92.1 2.8 %collective-permute-done.6 = f32[4,2,2048,2]{2,3,0,1:T(2,128)S(1)} collective-permute-done((f32[4,2,2048,2]{2,3,0,1:T(2,128)S(1)}, f32[4,2,2048,2]{2,3,0,1:T(2,128)S(1)}, u32[]{:S(2)}, u32[]{:S(2)}) %collective-permute-start.6) | collective-permute-done | bytes 131104 | tf_op jit(solution)/shard_map/ppermute | solution.py:23
  95.0 0.2 select_bitcast_fusion.2
  95.1 0.1 pad_maximum_fusion.2
  95.4 1.3 collective-permute-start.7
  96.6 2.9 %collective-permute-done.7 = f32[2,4,2048,2]{2,3,1,0:T(2,128)S(1)} collective-permute-done((f32[2,4,2048,2]{2,3,1,0:T(2,128)S(1)}, f32[2,4,2048,2]{2,3,1,0:T(2,128)S(1)}, u32[]{:S(2)}, u32[]{:S(2)}) %collective-permute-start.7) | collective-permute-done | bytes 131104 | tf_op jit(solution)/shard_map/ppermute | solution.py:23
  99.5 0.1 fusion.29
  99.7 0.1 pad_maximum_fusion.3
  99.8 0.1 select_bitcast_fusion
  100.0 5.2 %collective-permute-done.8 = f32[1,8,2048,2]{2,3,1,0:T(2,128)S(1)} collective-permute-done((f32[1,8,2048,2]{2,3,1,0:T(2,128)S(1)}, f32[1,8,2048,2]{2,3,1,0:T(2,128)S(1)}, u32[]{:S(2)}, u32[]{:S(2)}) %collective-permute-start.8) | collective-permute-done | bytes 131104 | tf_op jit(solution)/shard_map/ppermute | solution.py:23
  105.2 0.1 fusion.27
  105.3 0.1 pad_maximum_fusion.4
  105.4 0.2 copy.104
  105.6 0.6 fusion.32
  106.2 0.4 fusion
  106.6 1.0 pad_maximum_fusion
  107.6 16.7 %reduce-scatter.5.cloned.1.call-done = f32[128,3,256]{2,0,1:T(8,128)} async-done(((f32[256,3,256]{2,0,1:T(8,128)}), f32[128,3,256]{2,0,1:T(8,128)}) %reduce-scatter.5.cloned.1.call-update) | async-done | bytes 393232 | tf_op jit(solution)/shard_map/reduce_scatter | solution.py:156
  124.2 2.5 %convolution_bitcast_fusion = f32[3,128,256]{1,2,0:T(8,128)S(1)} fusion(f32[128,3,256]{2,0,1:T(8,128)} %reduce-scatter.5.cloned.1.call-done, f32[256]{0:T(256)S(1)} %multiply_add_fusion, f32[256]{0:T(256)S(1)} %convert_multiply_fusion, f32[256]{0:T(256)S(1)} %compare_select_fusion.2), kind=kOutput, calls=%fused_computation | convolution fusion | flops 302186496 | bytes 789504 | tf_op jit(solution)/shard_map/itk,kj->tij/dot_general | solution.py:159
  126.9 0.8 copy.107
  127.6 0.8 copy.106
  128.4 0.8 copy.105
  (53 shorter events, 1.1 us)
Async XLA Ops:
  7.2 1.1 copy-start
  7.2 22.7 %reduce-scatter.3.cloned.1.call-start = ((), (), s32[]{:S(2)}) async-start(), calls=%async_computation.2 | async-start | bytes 393216 | tf_op jit(solution)/shard_map/reduce_scatter | solution.py:112
  8.3 0.9 copy-start.1
  9.6 6.1 %collective-permute-start = (f32[128,256]{0,1:T(8,128)S(1)}, f32[128,256]{0,1:T(8,128)S(1)}, u32[]{:S(2)}, u32[]{:S(2)}) collective-permute-start(f32[128,256]{0,1:T(8,128)S(1)} %bitcast.293), channel_id=1, source_target_pairs={{0,2},{2,4},{4,6},{6,8},{8,10},{10,12},{12,14},{14,16},{16,18},{18... | collective-permute-start | bytes 393224 | tf_op jit(solution)/shard_map/ppermute | solution.py:29
  18.6 105.6 %reduce-scatter.5.cloned.1.call-start = ((), (), s32[]{:S(2)}) async-start(), calls=%async_computation.3 | async-start | bytes 1179648 | tf_op jit(solution)/shard_map/reduce_scatter | solution.py:156
  31.0 3.6 %collective-permute-start.1 = (f32[8,1,2048,1]{2,1,3,0:T(1,128)S(1)}, f32[8,1,2048,1]{2,1,3,0:T(1,128)S(1)}, u32[]{:S(2)}, u32[]{:S(2)}) collective-permute-start(f32[8,1,2048,1]{2,1,3,0:T(1,128)S(1)} %fusion.55), channel_id=1, source_target_pairs={{0,2},{2,0},{4,6},{6,4},{8,10},{10,8},{12,14},{14,12},{16,18},{18,... | collective-permute-start | bytes 196616 | tf_op jit(solution)/shard_map/ppermute | solution.py:23
  34.9 3.3 %collective-permute-start.2 = (f32[4,2,2048,1]{2,3,1,0:T(1,128)S(1)}, f32[4,2,2048,1]{2,3,1,0:T(1,128)S(1)}, u32[]{:S(2)}, u32[]{:S(2)}) collective-permute-start(f32[4,2,2048,1]{2,3,1,0:T(1,128)S(1)} %get-tuple-element.53), channel_id=1, source_target_pairs={{0,4},{4,0},{2,6},{6,2},{8,12},{12,8},{10,14},{14,10},{16,20},{20,... | collective-permute-start | bytes 196616 | tf_op jit(solution)/shard_map/ppermute | solution.py:23
  38.5 3.2 %collective-permute-start.3 = (f32[2,4,2048,1]{2,3,1,0:T(1,128)S(1)}, f32[2,4,2048,1]{2,3,1,0:T(1,128)S(1)}, u32[]{:S(2)}, u32[]{:S(2)}) collective-permute-start(f32[2,4,2048,1]{2,3,1,0:T(1,128)S(1)} %fusion.49), channel_id=1, source_target_pairs={{0,8},{8,0},{2,10},{10,2},{4,12},{12,4},{6,14},{14,6},{16,24},{24,... | collective-permute-start | bytes 196616 | tf_op jit(solution)/shard_map/ppermute | solution.py:23
  42.0 19.3 %collective-permute-start.4 = (f32[1,8,2048,1]{2,1,3,0:T(8,128)S(1)}, f32[1,8,2048,1]{2,1,3,0:T(8,128)S(1)}, u32[]{:S(2)}, u32[]{:S(2)}) collective-permute-start(f32[1,8,2048,1]{2,1,3,0:T(8,128)S(1)} %select_bitcast_fusion.3), channel_id=1, source_target_pairs={{0,16},{16,0},{2,18},{18,2},{4,20},{20,4},{6,22},{22,6},{8,24},{24... | collective-permute-start | bytes 196616 | tf_op jit(solution)/shard_map/ppermute | solution.py:23
  86.7 3.9 %collective-permute-start.5 = (f32[8,1,2048,2]{2,3,0,1:T(2,128)S(1)}, f32[8,1,2048,2]{2,3,0,1:T(2,128)S(1)}, u32[]{:S(2)}, u32[]{:S(2)}) collective-permute-start(f32[8,1,2048,2]{2,3,0,1:T(2,128)S(1)} %fusion.19), channel_id=1, source_target_pairs={{0,2},{2,0},{4,6},{6,4},{8,10},{10,8},{12,14},{14,12},{16,18},{18,... | collective-permute-start | bytes 393224 | tf_op jit(solution)/shard_map/ppermute | solution.py:23
  90.8 4.1 %collective-permute-start.6 = (f32[4,2,2048,2]{2,3,0,1:T(2,128)S(1)}, f32[4,2,2048,2]{2,3,0,1:T(2,128)S(1)}, u32[]{:S(2)}, u32[]{:S(2)}) collective-permute-start(f32[4,2,2048,2]{2,3,0,1:T(2,128)S(1)} %fusion.20), channel_id=1, source_target_pairs={{0,4},{4,0},{2,6},{6,2},{8,12},{12,8},{10,14},{14,10},{16,20},{20,... | collective-permute-start | bytes 393224 | tf_op jit(solution)/shard_map/ppermute | solution.py:23
  95.4 4.2 %collective-permute-start.7 = (f32[2,4,2048,2]{2,3,1,0:T(2,128)S(1)}, f32[2,4,2048,2]{2,3,1,0:T(2,128)S(1)}, u32[]{:S(2)}, u32[]{:S(2)}) collective-permute-start(f32[2,4,2048,2]{2,3,1,0:T(2,128)S(1)} %fusion.21), channel_id=1, source_target_pairs={{0,8},{8,0},{2,10},{10,2},{4,12},{12,4},{6,14},{14,6},{16,24},{24,... | collective-permute-start | bytes 393224 | tf_op jit(solution)/shard_map/ppermute | solution.py:23
  99.9 5.3 %collective-permute-start.8 = (f32[1,8,2048,2]{2,3,1,0:T(2,128)S(1)}, f32[1,8,2048,2]{2,3,1,0:T(2,128)S(1)}, u32[]{:S(2)}, u32[]{:S(2)}) collective-permute-start(f32[1,8,2048,2]{2,3,1,0:T(2,128)S(1)} %select_bitcast_fusion), channel_id=1, source_target_pairs={{0,16},{16,0},{2,18},{18,2},{4,20},{20,4},{6,22},{22,6},{8,24},{24... | collective-permute-start | bytes 393224 | tf_op jit(solution)/shard_map/ppermute | solution.py:23
Sparse Core Ops, SparseCore 0:
  18.7 11.1 reduce-scatter.2
  107.7 16.4 reduce-scatter.4
where the time goes:
time: 137 us; the launch traced here: 136 us
  other arithmetic  46.3 us (34%)
  waiting for transfers between devices  45.9 us (34%)
  starting transfers between devices  15.3 us (11%)
  between operations  14.6 us (11%)
  local copies, waits for them, and re-layouts  7.57 us (6%)
  matrix products  6.27 us (5%)
    div x2, other arithmetic, per_device(): lax.linalg.tridiagonal_solve(below_band, middle_band, above_band, series[...  29.9 us
    ppermute x8, waiting for transfers between devices, swapped(): return lax.ppermute(block, axis, route)  17.4 us
    reduce_scatter x1, waiting for transfers between devices, per_device(): lax.psum_scatter(jnp.concatenate([values, slopes], axis=1), 'space', scat...  16.7 us
    sub x1, other arithmetic, per_device(): lax.linalg.tridiagonal_solve(below_band, middle_band, above_band, series[...  11.3 us
    ppermute x8, starting transfers between devices, swapped(): return lax.ppermute(block, axis, route)  11.1 us
    reduce_scatter x1, waiting for transfers between devices, per_device(): lax.psum_scatter(jnp.einsum('ki,itj->ktj', both, column_modes, precision=...  10.8 us
    unnamed x27, local copies, waits for them, and re-layouts  4.51 us
    ppermute x1, starting transfers between devices, shifted(): return lax.ppermute(array, axis, pairs)  3.94 us
  transfers between devices with their start and end apart: 11, of which 10 were waited for; matrix products, arithmetic and copies ran while one was open for 14% of the time, Pallas kernels for 0%

commit v1 on v0

--- a/solution.py
+++ b/solution.py
@@ -1,6 +1,9 @@
 import jax
 import jax.numpy as jnp
+import numpy as np
 from jax import lax
+from jax.experimental import pallas as pl
+from jax.experimental.pallas import tpu as pltpu
 from jax.sharding import PartitionSpec as P
 
 NEWTON = 4
@@ -80,7 +83,7 @@
     return blocks
 
 
-def per_device(density, flux_x, flux_y):
+def per_device_xla(density, flux_x, flux_y):
     slabs = density.shape[0]
     rows_local = density.shape[1]
     count = density.shape[2]
@@ -169,6 +172,282 @@
     return (density_out, flux_x_out, flux_y_out)
 
 
+MESH = pl.DeviceIdType.MESH
+
+
+def split_table(table):
+    high = table.astype(jnp.bfloat16)
+    low = (table - high.astype(np.float32)).astype(jnp.bfloat16)
+    return np.stack([high, low], axis=-3)
+
+
+def host_tables(count, parts, solvers):
+    modes_local = count // parts
+    modes = np.arange(count, dtype=np.float64)[:, None]
+    points = np.arange(count, dtype=np.float64)[None, :]
+    table = np.cos(np.pi * modes * (2.0 * points + 1.0) / (2.0 * count))
+    table = table * np.where(modes == 0, np.sqrt(1.0 / count), np.sqrt(2.0 / count))
+    wide = np.concatenate([table] + [table[:, -1:]] * 8, axis=1)
+    forward, inverse, border = [], [], []
+    for own in range(parts):
+        mine = slice(own * modes_local, (own + 1) * modes_local)
+        order = [own, 1 - own]
+        forward.append(np.concatenate(
+            [table[mine, q * modes_local:(q + 1) * modes_local] for q in order], axis=1))
+        inverse.append(np.concatenate(
+            [wide[mine, q * modes_local:(q + 1) * modes_local + 8].T for q in order[::-1]], axis=0))
+        border.append(np.broadcast_to(
+            -flux_weight * table[mine, modes_local:modes_local + 1], (modes_local, 128)))
+    lam = 4.0 * np.sin(np.pi * np.arange(count) / (2.0 * count)) ** 2
+    coeff = 2.0 + regular_shift + space_weight * (lam[:, None] + lam[None, :])
+    rows = modes_local // solvers
+    f32 = np.float32
+    return (
+        split_table(table.T.astype(f32)),
+        split_table(table.astype(f32)),
+        split_table(np.stack(forward).astype(f32)),
+        split_table(np.stack(inverse).astype(f32)),
+        np.stack(border).astype(f32),
+        coeff.reshape(parts, solvers, rows, count).astype(f32),
+    )
+
+
+def parted(x):
+    high = x.astype(jnp.bfloat16)
+    return high, (x - high.astype(jnp.float32)).astype(jnp.bfloat16)
+
+
+def mul(a, b):
+    return jnp.dot(a, b, preferred_element_type=jnp.float32)
+
+
+def by_table(x, table):
+    high, low = parted(x)
+    return mul(high, table[0]) + (mul(high, table[1]) + mul(low, table[0]))
+
+
+def table_by(table, x):
+    high, low = parted(x)
+    return mul(table[0], high) + (mul(table[1], high) + mul(table[0], low))
+
+
+def step_kernel(
+    total, density, flux_x, flux_y, colf, coli, rowf, rowi, border, coeff,
+    out_d, out_x, out_y,
+    dv, xv, yv, rho, mx, my, colf_v, coli_v, rowf_v, rowi_v, border_v, coeff_v,
+    stack, ysend, yrecv, outgoing, incoming, pivots, phi, home, psend, pown, precv,
+    res_d, res_x, res_y,
+    load_sem, ex_send, ex_recv, out_send, out_recv, back_send, back_recv, fin_send, fin_recv,
+    store_sem,
+):
+    me = lax.axis_index("tm")
+    side = lax.axis_index("space")
+    rows, count = dv.shape
+    group = coeff_v.shape[0]
+    loads = [
+        pltpu.make_async_copy(src, dst, load_sem.at[i])
+        for i, (src, dst) in enumerate([
+            (density.at[0], dv), (flux_x.at[0], xv), (flux_y.at[0], yv),
+            (colf, colf_v), (rowf.at[side], rowf_v), (border.at[side], border_v),
+            (coeff.at[side, me], coeff_v), (coli, coli_v), (rowi.at[side], rowi_v),
+        ])
+    ]
+    for load in loads:
+        load.start()
+    near = sorted(range(1, total), key=lambda j: -min(j, total - j))
+    peers = [lax.rem(me + j, total) for j in near]
+    other = {"space": 1 - side}
+    barrier = pltpu.get_barrier_semaphore()
+    for peer in peers:
+        pl.semaphore_signal(barrier, inc=1, device_id={"tm": peer}, device_id_type=MESH)
+    pl.semaphore_signal(barrier, inc=1, device_id=other, device_id_type=MESH)
+
+    for load in loads[:3]:
+        load.wait()
+    tile = 16
+
+    def prox(i, carry):
+        span = pl.ds(pl.multiple_of(i * tile, tile), tile)
+        r, fx, fy = dv[span], xv[span], yv[span]
+        q, a, b = kinetic_prox(r, fx, fy)
+        rho[span] = q
+        mx[span] = a
+        my[span] = b
+        return carry
+
+    lax.fori_loop(0, rows // tile, prox, 0)
+    loads[3].wait()
+
+    def exchange(lo, size, k):
+        span = pl.ds(lo, size)
+        return pltpu.make_async_remote_copy(
+            src_ref=ysend.at[span], dst_ref=yrecv.at[span], send_sem=ex_send.at[k],
+            recv_sem=ex_recv.at[k], device_id=other, device_id_type=MESH)
+
+    ysend[:rows] = by_table(rho[...], colf_v)
+    pl.semaphore_wait(barrier, total)
+    swap_rho = exchange(0, rows, 0)
+    swap_rho.start()
+    row = lax.broadcasted_iota(jnp.int32, (rows, count), 0)
+    col = lax.broadcasted_iota(jnp.int32, (rows, count), 1)
+    last = side * rows + row == 2 * rows - 1
+    wx = jnp.where(last, 0.0, mx[...])
+    wy = jnp.where(col == count - 1, 0.0, my[...])
+    div = wx - jnp.where(row == 0, 0.0, pltpu.roll(wx, 1, 0)) + wy - pltpu.roll(wy, 1, 1)
+    stack[:rows] = flux_weight * div
+    stack[rows:] = wx[rows - 8:]
+    ysend[rows:] = by_table(stack[...], colf_v)
+    swap_div = exchange(rows, rows + 8, 1)
+    swap_div.start()
+
+    def outward(field, peer):
+        return pltpu.make_async_remote_copy(
+            src_ref=outgoing.at[field, peer], dst_ref=incoming.at[field, me],
+            send_sem=out_send.at[field, peer], recv_sem=out_recv.at[field, me],
+            device_id={"tm": peer}, device_id_type=MESH)
+
+    def arrival(field, peer):
+        return pltpu.make_async_remote_copy(
+            src_ref=outgoing.at[field, peer], dst_ref=incoming.at[field, peer],
+            send_sem=out_send.at[field, peer], recv_sem=out_recv.at[field, peer],
+            device_id={"tm": peer}, device_id_type=MESH)
+
+    loads[4].wait()
+    loads[5].wait()
+    swap_rho.wait_recv()
+    both = jnp.concatenate([ysend[:rows], yrecv[:rows]], axis=0)
+    outgoing[0] = table_by(rowf_v, both).reshape(total, group, count)
+    for peer in peers:
+        outward(0, peer).start()
+    swap_div.wait_recv()
+    both = jnp.concatenate([ysend[rows:2 * rows], yrecv[rows:2 * rows]], axis=0)
+    halo = ysend[2 * rows + 7:2 * rows + 8] + yrecv[2 * rows + 7:2 * rows + 8]
+    modal = table_by(rowf_v, both) + border_v[:, :1] * halo
+    outgoing[1] = modal.reshape(total, group, count)
+    for peer in peers:
+        outward(1, peer).start()
+    incoming[0, me] = outgoing[0, me]
+    incoming[1, me] = outgoing[1, me]
+    loads[6].wait()
+    c = coeff_v[...]
+    pivot = 1.0 / c
+    pivots[0] = pivot
+    for t in range(1, total):
+        pivot = 1.0 / (c - pivot)
+        pivots[t] = pivot
+    for load in loads[7:]:
+        load.wait()
+    for peer in peers:
+        arrival(0, peer).wait_recv()
+        arrival(1, peer).wait_recv()
+    phi[total] = jnp.zeros_like(c)
+    value = (incoming[0, 0] + incoming[1, 0]) * pivots[0]
+    phi[0] = value
+    for t in range(1, total):
+        value = (incoming[0, t] - incoming[0, t - 1] + incoming[1, t] + value) * pivots[t]
+        phi[t] = value
+    for t in reversed(range(total - 1)):
+        value = phi[t] + pivots[t] * value
+        phi[t] = value
+
+    def homeward(peer, block):
+        return pltpu.make_async_remote_copy(
+            src_ref=phi.at[pl.ds(peer, 2)], dst_ref=home.at[block],
+            send_sem=back_send.at[peer], recv_sem=back_recv.at[block],
+            device_id={"tm": peer}, device_id_type=MESH)
+
+    for peer in peers:
+        homeward(peer, me).start()
+    home[me, 0] = phi[me]
+    home[me, 1] = phi[me + 1]
+    for peer in peers:
+        homeward(peer, peer).wait_recv()
+
+    def final(k):
+        return pltpu.make_async_remote_copy(
+            src_ref=psend.at[k], dst_ref=precv.at[k], send_sem=fin_send.at[k],
+            recv_sem=fin_recv.at[k], device_id=other, device_id_type=MESH)
+
+    finals = [final(0), final(1)]
+    for k in range(2):
+        modes = home[:, k].reshape(rows, count)
+        part = by_table(modes, coli_v)
+        whole = table_by(rowi_v, part)
+        psend[k] = whole[:rows + 8]
+        finals[k].start()
+        pown[k] = whole[rows + 8:]
+    finals[0].wait_recv()
+    pot = pown[0] + precv[0]
+    here = pot[:rows]
+    grad = pltpu.roll(pot, rows + 7, 0)[:rows] - here
+    res_x[...] = mx[...] - flux_weight * grad
+    save_x = pltpu.make_async_copy(res_x, out_x.at[0], store_sem.at[0])
+    save_x.start()
+    grad = jnp.where(col == count - 1, 0.0, pltpu.roll(here, count - 1, 1) - here)
+    res_y[...] = my[...] - flux_weight * grad
+    save_y = pltpu.make_async_copy(res_y, out_y.at[0], store_sem.at[1])
+    save_y.start()
+    finals[1].wait_recv()
+    res_d[...] = rho[...] - (here - (pown[1, :rows] + precv[1, :rows]))
+    save_d = pltpu.make_async_copy(res_d, out_d.at[0], store_sem.at[2])
+    save_d.start()
+    swap_rho.wait_send()
+    swap_div.wait_send()
+    for peer in peers:
+        outward(0, peer).wait_send()
+        outward(1, peer).wait_send()
+        homeward(peer, me).wait_send()
+    for copy in finals:
+        copy.wait_send()
+    for save in (save_x, save_y, save_d):
+        save.wait()
+
+
+def per_device_kernel(density, flux_x, flux_y):
+    rows, count = density.shape[1:]
+    parts = lax.axis_size("space")
+    total = lax.axis_size("tm")
+    group = rows // total
+    tables = host_tables(count, parts, total)
+    f32, bf16 = jnp.float32, jnp.bfloat16
+    vm = pltpu.VMEM
+    dma = pltpu.SemaphoreType.DMA
+    slab = vm((rows, count), f32)
+    scratch = [slab] * 6 + [
+        vm((2, count, count), bf16), vm((2, count, count), bf16),
+        vm((2, rows, count), bf16), vm((2, 2 * (rows + 8), rows), bf16),
+        vm((rows, 128), f32), vm((group, count), f32),
+        vm((rows + 8, count), f32), vm((2 * rows + 8, count), f32), vm((2 * rows + 8, count), f32),
+        vm((2, total, group, count), f32), vm((2, total, group, count), f32),
+        vm((total, group, count), f32), vm((total + 1, group, count), f32),
+        vm((total, 2, group, count), f32),
+        vm((2, rows + 8, count), f32), vm((2, rows + 8, count), f32), vm((2, rows + 8, count), f32),
+        slab, slab, slab,
+        dma((9,)), dma((2,)), dma((2,)), dma((2, total)), dma((2, total)),
+        dma((total,)), dma((total,)), dma((2,)), dma((2,)), dma((3,)),
+    ]
+    anywhere = pl.BlockSpec(memory_space=pl.ANY)
+
+    def kernel(*refs):
+        step_kernel(total, *refs)
+
+    return pl.pallas_call(
+        kernel,
+        out_shape=[jax.ShapeDtypeStruct(density.shape, f32)] * 3,
+        in_specs=[anywhere] * 9,
+        out_specs=[anywhere] * 3,
+        scratch_shapes=scratch,
+        compiler_params=pltpu.CompilerParams(collective_id=0, has_side_effects=True),
+    )(density, flux_x, flux_y, *tables)
+
+
+def per_device(density, flux_x, flux_y):
+    slabs, rows, count = density.shape
+    fits = slabs == 1 and lax.axis_size("space") == 2 and rows % (8 * lax.axis_size("tm")) == 0
+    return (per_device_kernel if fits and count % 128 == 0 else per_device_xla)(
+        density, flux_x, flux_y)
+
+
 def solution(mesh):
     return jax.shard_map(
         per_device,

time: 137 us -> 32.1 us (0.23)
  other arithmetic: 46.3 us -> 0 us
  waiting for transfers between devices: 45.9 us -> 0 us
  Pallas kernels: 0 us -> 28.1 us
  starting transfers between devices: 15.3 us -> 0 us
  between operations: 14.6 us -> 0.65 us
  matrix products: 6.27 us -> 0 us
  local copies, waits for them, and re-layouts: 7.57 us -> 3.21 us
    div x2 -> x0, other arithmetic: 29.9 us -> none  [per_device(): lax.linalg.tridiagonal_solve(below_band, middle_band, above_band, series[...]
    pallas_call x0 -> x1, Pallas kernels: none -> 28.1 us  [per_device_kernel(): pl.pallas_call(kernel, out_shape=[jax.ShapeDtypeStruct(density.shape, f32...]
    reduce_scatter x2 -> x0, waiting for transfers between devices: 27.4 us -> none  [the longest x1 16.7 us: per_device(): lax.psum_scatter(jnp.concatenate([values, slopes], axis=1), 'space', scat...]
    ppermute x9 -> x0, waiting for transfers between devices: 18.4 us -> none  [the longest x8 17.4 us: swapped(): return lax.ppermute(block, axis, route)]
    ppermute x9 -> x0, starting transfers between devices: 15 us -> none  [the longest x8 11.1 us: swapped(): return lax.ppermute(block, axis, route)]
    sub x5 -> x0, other arithmetic: 11.4 us -> none  [the longest x1 11.3 us: per_device(): lax.linalg.tridiagonal_solve(below_band, middle_band, above_band, series[...]
    dot_general x5 -> x0, matrix products: 6.27 us -> none  [the longest x1 2.54 us: per_device(): physical = jnp.einsum('itk,kj->tij', gathered, table, precision=highest)]
    slice x6 -> x0, local copies, waits for them, and re-layouts: 1.51 us -> none  [the longest x4 1.49 us: per_device(): lax.linalg.tridiagonal_solve(below_band, middle_band, above_band, series[...]
  transfers between devices with their start and end apart: 11 -> 0, of which waited for: 10 -> 0; matrix products, arithmetic and copies ran while one was open for 14% -> 0% of each run, Pallas kernels for 0% -> 0%
where the time goes in v1:
time: 32.1 us; the launch traced here: 31.9 us
  Pallas kernels  28.1 us (88%)
  local copies, waits for them, and re-layouts  3.21 us (10%)
  between operations  0.65 us (2%)
    pallas_call x1, Pallas kernels, per_device_kernel(): pl.pallas_call(kernel, out_shape=[jax.ShapeDtypeStruct(density.shape, f32...  28.1 us
    unnamed x7, local copies, waits for them, and re-layouts  3.21 us

profile of v1, /device:TPU:1, one launch (start us, length us, event | category | flops | bytes accessed | tf_op | source)
XLA Modules:
  0.0 31.9 jit_solution(4776784690335191890)
XLA Ops:
  0.6 28.1 %shard_map.112 = (f32[1,128,256]{2,1,0:T(8,128)}, f32[1,128,256]{2,1,0:T(8,128)}, f32[1,128,256]{2,1,0:T(8,128)}) custom-call(f32[1,128,256]{2,1,0:T(8,128)} %refs_0_.1, f32[1,128,256]{2,1,0:T(8,128)} %refs_1_.1, f32[1,128,256]{2,1,0:T(8,128)} %refs_2_.1, bf16[2,256,256]{2,1,0:T(8,128)(2,1)} %constant.12.clone.refs_3_, ...), custom_call_target="tpu_custom_call" | custom-call | tf_op jit(solution)/shard_map/pallas_call | solution.py:434
  28.7 0.0 copy-start.1
  28.7 1.6 %copy.15 = f32[1,128,256]{2,1,0:T(8,128)} copy(f32[1,128,256]{2,1,0:T(8,128)} %get-tuple-element.6) | data formatting | bytes 262144
  30.3 0.0 copy-done.1
  30.3 0.0 copy-start
  30.3 0.7 %copy.16 = f32[1,128,256]{2,1,0:T(8,128)} copy(f32[1,128,256]{2,1,0:T(8,128)S(1)} %copy-done.1) | data formatting | bytes 262144
  31.0 0.3 copy-done
  31.3 0.7 %copy.17 = f32[1,128,256]{2,1,0:T(8,128)} copy(f32[1,128,256]{2,1,0:T(8,128)S(1)} %copy-done) | data formatting | bytes 262144
Async XLA Ops:
  28.7 1.6 %copy-start.1 = (f32[1,128,256]{2,1,0:T(8,128)S(1)}, f32[1,128,256]{2,1,0:T(8,128)}, u32[]{:S(2)}) copy-start(f32[1,128,256]{2,1,0:T(8,128)} %get-tuple-element.7) | copy-start | bytes 393220
  30.3 1.0 %copy-start = (f32[1,128,256]{2,1,0:T(8,128)S(1)}, f32[1,128,256]{2,1,0:T(8,128)}, u32[]{:S(2)}) copy-start(f32[1,128,256]{2,1,0:T(8,128)} %get-tuple-element.8) | copy-start | bytes 393220

commit v2 on v1

--- a/solution.py
+++ b/solution.py
@@ -233,12 +233,10 @@
 
 def step_kernel(
     total, density, flux_x, flux_y, colf, coli, rowf, rowi, border, coeff,
-    out_d, out_x, out_y,
-    dv, xv, yv, rho, mx, my, colf_v, coli_v, rowf_v, rowi_v, border_v, coeff_v,
-    stack, ysend, yrecv, outgoing, incoming, pivots, phi, home, psend, pown, precv,
-    res_d, res_x, res_y,
+    rho, mx, my, pown, precv,
+    dv, xv, yv, colf_v, coli_v, rowf_v, rowi_v, border_v, coeff_v,
+    stack, ysend, yrecv, outgoing, incoming, pivots, phi, home, psend,
     load_sem, ex_send, ex_recv, out_send, out_recv, back_send, back_recv, fin_send, fin_recv,
-    store_sem,
 ):
     me = lax.axis_index("tm")
     side = lax.axis_index("space")
@@ -377,6 +375,20 @@
         finals[k].start()
         pown[k] = whole[rows + 8:]
     finals[0].wait_recv()
+    finals[1].wait_recv()
+    swap_rho.wait_send()
+    swap_div.wait_send()
+    for peer in peers:
+        outward(0, peer).wait_send()
+        outward(1, peer).wait_send()
+        homeward(peer, me).wait_send()
+    for copy in finals:
+        copy.wait_send()
+
+
+def finish_kernel(rho, mx, my, pown, precv, out_d, out_x, out_y, res_d, res_x, res_y, store_sem):
+    rows, count = rho.shape
+    col = lax.broadcasted_iota(jnp.int32, (rows, count), 1)
     pot = pown[0] + precv[0]
     here = pot[:rows]
     grad = pltpu.roll(pot, rows + 7, 0)[:rows] - here
@@ -387,18 +399,9 @@
     res_y[...] = my[...] - flux_weight * grad
     save_y = pltpu.make_async_copy(res_y, out_y.at[0], store_sem.at[1])
     save_y.start()
-    finals[1].wait_recv()
     res_d[...] = rho[...] - (here - (pown[1, :rows] + precv[1, :rows]))
     save_d = pltpu.make_async_copy(res_d, out_d.at[0], store_sem.at[2])
     save_d.start()
-    swap_rho.wait_send()
-    swap_div.wait_send()
-    for peer in peers:
-        outward(0, peer).wait_send()
-        outward(1, peer).wait_send()
-        homeward(peer, me).wait_send()
-    for copy in finals:
-        copy.wait_send()
     for save in (save_x, save_y, save_d):
         save.wait()
 
@@ -413,7 +416,7 @@
     vm = pltpu.VMEM
     dma = pltpu.SemaphoreType.DMA
     slab = vm((rows, count), f32)
-    scratch = [slab] * 6 + [
+    scratch = [slab] * 3 + [
         vm((2, count, count), bf16), vm((2, count, count), bf16),
         vm((2, rows, count), bf16), vm((2, 2 * (rows + 8), rows), bf16),
         vm((rows, 128), f32), vm((group, count), f32),
@@ -421,24 +424,32 @@
         vm((2, total, group, count), f32), vm((2, total, group, count), f32),
         vm((total, group, count), f32), vm((total + 1, group, count), f32),
         vm((total, 2, group, count), f32),
-        vm((2, rows + 8, count), f32), vm((2, rows + 8, count), f32), vm((2, rows + 8, count), f32),
-        slab, slab, slab,
+        vm((2, rows + 8, count), f32),
         dma((9,)), dma((2,)), dma((2,)), dma((2, total)), dma((2, total)),
-        dma((total,)), dma((total,)), dma((2,)), dma((2,)), dma((3,)),
+        dma((total,)), dma((total,)), dma((2,)), dma((2,)),
     ]
     anywhere = pl.BlockSpec(memory_space=pl.ANY)
 
     def kernel(*refs):
         step_kernel(total, *refs)
 
-    return pl.pallas_call(
+    local = pl.BlockSpec(memory_space=pltpu.VMEM)
+    pair = vm((2, rows + 8, count), f32)
+    held = pl.pallas_call(
         kernel,
-        out_shape=[jax.ShapeDtypeStruct(density.shape, f32)] * 3,
+        out_shape=[slab, slab, slab, pair, pair],
         in_specs=[anywhere] * 9,
-        out_specs=[anywhere] * 3,
+        out_specs=[local] * 5,
         scratch_shapes=scratch,
         compiler_params=pltpu.CompilerParams(collective_id=0, has_side_effects=True),
     )(density, flux_x, flux_y, *tables)
+    return pl.pallas_call(
+        finish_kernel,
+        out_shape=[jax.ShapeDtypeStruct(density.shape, f32)] * 3,
+        in_specs=[local] * 5,
+        out_specs=[anywhere] * 3,
+        scratch_shapes=[slab, slab, slab, dma((3,))],
+    )(*[pltpu.with_memory_space_constraint(x, pltpu.VMEM) for x in held])
 
 
 def per_device(density, flux_x, flux_y):

time: 32.1 us -> 29.1 us (0.907)
  local copies, waits for them, and re-layouts: 3.21 us -> 0 us
    unnamed x7 -> x0, local copies, waits for them, and re-layouts: 3.21 us -> none
    pallas_call x1 -> x2, Pallas kernels: 28.1 us -> 28.3 us  [the longest x1 27.4 us: per_device_kernel(): pl.pallas_call(kernel, out_shape=[slab, slab, slab, pair, pair], in_specs...]
where the time goes in v2:
time: 29.1 us; the launch traced here: 28.9 us
  Pallas kernels  28.3 us (97%)
  between operations  0.64 us (2%)
    pallas_call x1, Pallas kernels, per_device_kernel(): pl.pallas_call(kernel, out_shape=[slab, slab, slab, pair, pair], in_specs...  27.4 us
    pallas_call x1, Pallas kernels, per_device_kernel(): pl.pallas_call(finish_kernel, out_shape=[jax.ShapeDtypeStruct(density.sha...  0.85 us

profile of v2, /device:TPU:1, one launch (start us, length us, event | category | flops | bytes accessed | tf_op | source)
XLA Modules:
  0.0 28.9 jit_solution(18391222056768019761)
XLA Ops:
  0.6 27.4 %shard_map.112 = (f32[128,256]{1,0:T(8,128)S(1)}, f32[128,256]{1,0:T(8,128)S(1)}, f32[128,256]{1,0:T(8,128)S(1)}, f32[2,136,256]{2,1,0:T(8,128)S(1)}, f32[2,136,256]{2,1,0:T(8,128)S(1)}) custom-call(f32[1,128,256]{2,1,0:T(8,128)} %refs_0_.1, f32[1,128,256]{2,1,0:T(8,128)} %refs_1_.1, f32[1,128,256]{2,1,0:T(8,128)} %refs_2_.1, ...), custom_call_target="tpu_custom_call" | custom-call | tf_op jit(solution)/shard_map/pallas_call | solution.py:438
  28.1 0.8 %shard_map.113 = (f32[1,128,256]{2,1,0:T(8,128)}, f32[1,128,256]{2,1,0:T(8,128)}, f32[1,128,256]{2,1,0:T(8,128)}) custom-call(f32[128,256]{1,0:T(8,128)S(1)} %get-tuple-element.8.rho, f32[128,256]{1,0:T(8,128)S(1)} %get-tuple-element.9.mx, f32[128,256]{1,0:T(8,128)S(1)} %get-tuple-element.10.my, f32[2,136,256]{2,1,0:T(8,128)S(1)} %get-tuple-element.11.pown, ...), custom_call_target="tpu_custom_call" | custom-call | tf_op jit(solution)/shard_map/pallas_call | solution.py:446

commit v3 on v2

--- a/solution.py
+++ b/solution.py
@@ -235,10 +235,14 @@
     total, density, flux_x, flux_y, colf, coli, rowf, rowi, border, coeff,
     rho, mx, my, pown, precv,
     dv, xv, yv, colf_v, coli_v, rowf_v, rowi_v, border_v, coeff_v,
-    stack, ysend, yrecv, outgoing, incoming, pivots, phi, home, psend,
-    load_sem, ex_send, ex_recv, out_send, out_recv, back_send, back_recv, fin_send, fin_recv,
+    stack, ysend, yrecv, outgoing, incoming, pivots, phi, home, psend, steps, cut,
+    load_sem, ex_send, ex_recv, out_send, out_recv, back_send, back_recv, fin_send, fin_recv, cut_sem,
 ):
-    me = lax.axis_index("tm")
+    place = lax.axis_index("tm")
+    half = place // total
+    me = place - half * total
+    base = half * total
+    mirror = {"tm": lax.rem(place + total, 2 * total)}
     side = lax.axis_index("space")
     rows, count = dv.shape
     group = coeff_v.shape[0]
@@ -257,7 +261,8 @@
     other = {"space": 1 - side}
     barrier = pltpu.get_barrier_semaphore()
     for peer in peers:
-        pl.semaphore_signal(barrier, inc=1, device_id={"tm": peer}, device_id_type=MESH)
+        pl.semaphore_signal(barrier, inc=1, device_id={"tm": base + peer}, device_id_type=MESH)
+    pl.semaphore_signal(barrier, inc=1, device_id=mirror, device_id_type=MESH)
     pl.semaphore_signal(barrier, inc=1, device_id=other, device_id_type=MESH)
 
     for load in loads[:3]:
@@ -283,7 +288,7 @@
             recv_sem=ex_recv.at[k], device_id=other, device_id_type=MESH)
 
     ysend[:rows] = by_table(rho[...], colf_v)
-    pl.semaphore_wait(barrier, total)
+    pl.semaphore_wait(barrier, total + 1)
     swap_rho = exchange(0, rows, 0)
     swap_rho.start()
     row = lax.broadcasted_iota(jnp.int32, (rows, count), 0)
@@ -302,13 +307,13 @@
         return pltpu.make_async_remote_copy(
             src_ref=outgoing.at[field, peer], dst_ref=incoming.at[field, me],
             send_sem=out_send.at[field, peer], recv_sem=out_recv.at[field, me],
-            device_id={"tm": peer}, device_id_type=MESH)
+            device_id={"tm": base + peer}, device_id_type=MESH)
 
     def arrival(field, peer):
         return pltpu.make_async_remote_copy(
             src_ref=outgoing.at[field, peer], dst_ref=incoming.at[field, peer],
             send_sem=out_send.at[field, peer], recv_sem=out_recv.at[field, peer],
-            device_id={"tm": peer}, device_id_type=MESH)
+            device_id={"tm": base + peer}, device_id_type=MESH)
 
     loads[4].wait()
     loads[5].wait()
@@ -333,26 +338,41 @@
     for t in range(1, total):
         pivot = 1.0 / (c - pivot)
         pivots[t] = pivot
+    inverse = 1.0 / (1.0 - pivot * pivot)
     for load in loads[7:]:
         load.wait()
     for peer in peers:
         arrival(0, peer).wait_recv()
         arrival(1, peer).wait_recv()
-    phi[total] = jnp.zeros_like(c)
-    value = (incoming[0, 0] + incoming[1, 0]) * pivots[0]
-    phi[0] = value
+    right = jnp.full(c.shape, half, jnp.int32) == 1
+    start, stride = half * (total - 1), 1 - 2 * half
+    steps[0] = incoming[0, 0] + incoming[1, 0]
     for t in range(1, total):
-        value = (incoming[0, t] - incoming[0, t - 1] + incoming[1, t] + value) * pivots[t]
-        phi[t] = value
-    for t in reversed(range(total - 1)):
-        value = phi[t] + pivots[t] * value
-        phi[t] = value
+        steps[t] = incoming[0, t] - incoming[0, t - 1] + incoming[1, t]
+    value = jnp.zeros_like(c)
+    for i in range(total):
+        value = (steps[start + stride * i] + value) * pivots[i]
+        steps[start + stride * i] = value
+    edge = jnp.where(right, 0.0, incoming[0, total - 1])
+    cut[0] = value - edge
+    swap = pltpu.make_async_remote_copy(
+        src_ref=cut.at[0], dst_ref=cut.at[1], send_sem=cut_sem.at[0], recv_sem=cut_sem.at[1],
+        device_id=mirror, device_id_type=MESH)
+    swap.start()
+    swap.wait_recv()
+    beyond = cut[1] - pivot * edge
+    value = (value + pivot * beyond) * inverse
+    phi[total] = jnp.where(right, 0.0, beyond + pivot * value)
+    phi[start + stride * (total - 1)] = value
+    for i in reversed(range(total - 1)):
+        value = steps[start + stride * i] + pivots[i] * value
+        phi[start + stride * i] = value
 
     def homeward(peer, block):
         return pltpu.make_async_remote_copy(
             src_ref=phi.at[pl.ds(peer, 2)], dst_ref=home.at[block],
             send_sem=back_send.at[peer], recv_sem=back_recv.at[block],
-            device_id={"tm": peer}, device_id_type=MESH)
+            device_id={"tm": base + peer}, device_id_type=MESH)
 
     for peer in peers:
         homeward(peer, me).start()
@@ -384,6 +404,7 @@
         homeward(peer, me).wait_send()
     for copy in finals:
         copy.wait_send()
+    swap.wait_send()
 
 
 def finish_kernel(rho, mx, my, pown, precv, out_d, out_x, out_y, res_d, res_x, res_y, store_sem):
@@ -409,7 +430,7 @@
 def per_device_kernel(density, flux_x, flux_y):
     rows, count = density.shape[1:]
     parts = lax.axis_size("space")
-    total = lax.axis_size("tm")
+    total = lax.axis_size("tm") // 2
     group = rows // total
     tables = host_tables(count, parts, total)
     f32, bf16 = jnp.float32, jnp.bfloat16
@@ -424,9 +445,9 @@
         vm((2, total, group, count), f32), vm((2, total, group, count), f32),
         vm((total, group, count), f32), vm((total + 1, group, count), f32),
         vm((total, 2, group, count), f32),
-        vm((2, rows + 8, count), f32),
+        vm((2, rows + 8, count), f32), vm((total, group, count), f32), vm((2, group, count), f32),
         dma((9,)), dma((2,)), dma((2,)), dma((2, total)), dma((2, total)),
-        dma((total,)), dma((total,)), dma((2,)), dma((2,)),
+        dma((total,)), dma((total,)), dma((2,)), dma((2,)), dma((2,)),
     ]
     anywhere = pl.BlockSpec(memory_space=pl.ANY)
 
@@ -454,7 +475,8 @@
 
 def per_device(density, flux_x, flux_y):
     slabs, rows, count = density.shape
-    fits = slabs == 1 and lax.axis_size("space") == 2 and rows % (8 * lax.axis_size("tm")) == 0
+    size = lax.axis_size("tm")
+    fits = slabs == 1 and lax.axis_size("space") == 2 and size % 2 == 0 and rows % (4 * size) == 0
     return (per_device_kernel if fits and count % 128 == 0 else per_device_xla)(
         density, flux_x, flux_y)
 

time: 29.1 us -> 25.1 us (0.86)
  Pallas kernels: 28.3 us -> 24.3 us
    pallas_call x1, Pallas kernels: 27.4 us -> 23.4 us  [per_device_kernel(): pl.pallas_call(kernel, out_shape=[slab, slab, slab, pair, pair], in_specs...]
where the time goes in v3:
time: 25.1 us; the launch traced here: 24.9 us
  Pallas kernels  24.3 us (97%)
  between operations  0.64 us (3%)
    pallas_call x1, Pallas kernels, per_device_kernel(): pl.pallas_call(kernel, out_shape=[slab, slab, slab, pair, pair], in_specs...  23.4 us
    pallas_call x1, Pallas kernels, per_device_kernel(): pl.pallas_call(finish_kernel, out_shape=[jax.ShapeDtypeStruct(density.sha...  0.85 us

profile of v3, /device:TPU:1, one launch (start us, length us, event | category | flops | bytes accessed | tf_op | source)
XLA Modules:
  0.0 24.9 jit_solution(5363611558011706385)
XLA Ops:
  0.6 23.4 %shard_map.112 = (f32[128,256]{1,0:T(8,128)S(1)}, f32[128,256]{1,0:T(8,128)S(1)}, f32[128,256]{1,0:T(8,128)S(1)}, f32[2,136,256]{2,1,0:T(8,128)S(1)}, f32[2,136,256]{2,1,0:T(8,128)S(1)}) custom-call(f32[1,128,256]{2,1,0:T(8,128)} %refs_0_.1, f32[1,128,256]{2,1,0:T(8,128)} %refs_1_.1, f32[1,128,256]{2,1,0:T(8,128)} %refs_2_.1, ...), custom_call_target="tpu_custom_call" | custom-call | tf_op jit(solution)/shard_map/pallas_call | solution.py:459
  24.0 0.8 %shard_map.113 = (f32[1,128,256]{2,1,0:T(8,128)}, f32[1,128,256]{2,1,0:T(8,128)}, f32[1,128,256]{2,1,0:T(8,128)}) custom-call(f32[128,256]{1,0:T(8,128)S(1)} %get-tuple-element.8.rho, f32[128,256]{1,0:T(8,128)S(1)} %get-tuple-element.9.mx, f32[128,256]{1,0:T(8,128)S(1)} %get-tuple-element.10.my, f32[2,136,256]{2,1,0:T(8,128)S(1)} %get-tuple-element.11.pown, ...), custom_call_target="tpu_custom_call" | custom-call | tf_op jit(solution)/shard_map/pallas_call | solution.py:467

commit v4 on v3

--- a/solution.py
+++ b/solution.py
@@ -173,6 +173,7 @@
 
 
 MESH = pl.DeviceIdType.MESH
+CHUNKS = 2
 
 
 def split_table(table):
@@ -195,7 +196,8 @@
         forward.append(np.concatenate(
             [table[mine, q * modes_local:(q + 1) * modes_local] for q in order], axis=1))
         inverse.append(np.concatenate(
-            [wide[mine, q * modes_local:(q + 1) * modes_local + 8].T for q in order[::-1]], axis=0))
+            [wide[q * modes_local:(q + 1) * modes_local,
+                  own * modes_local:(own + 1) * modes_local + 8].T for q in order], axis=1))
         border.append(np.broadcast_to(
             -flux_weight * table[mine, modes_local:modes_local + 1], (modes_local, 128)))
     lam = 4.0 * np.sin(np.pi * np.arange(count) / (2.0 * count)) ** 2
@@ -233,9 +235,9 @@
 
 def step_kernel(
     total, density, flux_x, flux_y, colf, coli, rowf, rowi, border, coeff,
-    rho, mx, my, pown, precv,
+    rho, mx, my, fields,
     dv, xv, yv, colf_v, coli_v, rowf_v, rowi_v, border_v, coeff_v,
-    stack, ysend, yrecv, outgoing, incoming, pivots, phi, home, psend, steps, cut,
+    stack, ysend, yrecv, outgoing, incoming, pivots, phi, home, across, steps, cut,
     load_sem, ex_send, ex_recv, out_send, out_recv, back_send, back_recv, fin_send, fin_recv, cut_sem,
 ):
     place = lax.axis_index("tm")
@@ -246,6 +248,7 @@
     side = lax.axis_index("space")
     rows, count = dv.shape
     group = coeff_v.shape[0]
+    part = group // CHUNKS
     loads = [
         pltpu.make_async_copy(src, dst, load_sem.at[i])
         for i, (src, dst) in enumerate([
@@ -303,16 +306,18 @@
     swap_div = exchange(rows, rows + 8, 1)
     swap_div.start()
 
-    def outward(field, peer):
+    def outward(field, k, peer):
+        span = pl.ds(k * part, part)
         return pltpu.make_async_remote_copy(
-            src_ref=outgoing.at[field, peer], dst_ref=incoming.at[field, me],
-            send_sem=out_send.at[field, peer], recv_sem=out_recv.at[field, me],
+            src_ref=outgoing.at[field, peer, span], dst_ref=incoming.at[field, me, span],
+            send_sem=out_send.at[field, k, peer], recv_sem=out_recv.at[field, k, me],
             device_id={"tm": base + peer}, device_id_type=MESH)
 
-    def arrival(field, peer):
+    def arrival(field, k, peer):
+        span = pl.ds(k * part, part)
         return pltpu.make_async_remote_copy(
-            src_ref=outgoing.at[field, peer], dst_ref=incoming.at[field, peer],
-            send_sem=out_send.at[field, peer], recv_sem=out_recv.at[field, peer],
+            src_ref=outgoing.at[field, peer, span], dst_ref=incoming.at[field, peer, span],
+            send_sem=out_send.at[field, k, peer], recv_sem=out_recv.at[field, k, peer],
             device_id={"tm": base + peer}, device_id_type=MESH)
 
     loads[4].wait()
@@ -321,14 +326,15 @@
     both = jnp.concatenate([ysend[:rows], yrecv[:rows]], axis=0)
     outgoing[0] = table_by(rowf_v, both).reshape(total, group, count)
     for peer in peers:
-        outward(0, peer).start()
+        outward(0, 0, peer).start()
     swap_div.wait_recv()
     both = jnp.concatenate([ysend[rows:2 * rows], yrecv[rows:2 * rows]], axis=0)
     halo = ysend[2 * rows + 7:2 * rows + 8] + yrecv[2 * rows + 7:2 * rows + 8]
     modal = table_by(rowf_v, both) + border_v[:, :1] * halo
     outgoing[1] = modal.reshape(total, group, count)
-    for peer in peers:
-        outward(1, peer).start()
+    for field, k in ((1, 0), (0, 1), (1, 1)):
+        for peer in peers:
+            outward(field, k, peer).start()
     incoming[0, me] = outgoing[0, me]
     incoming[1, me] = outgoing[1, me]
     loads[6].wait()
@@ -341,76 +347,92 @@
     inverse = 1.0 / (1.0 - pivot * pivot)
     for load in loads[7:]:
         load.wait()
-    for peer in peers:
-        arrival(0, peer).wait_recv()
-        arrival(1, peer).wait_recv()
-    right = jnp.full(c.shape, half, jnp.int32) == 1
+    right = jnp.full((part, count), half, jnp.int32) == 1
     start, stride = half * (total - 1), 1 - 2 * half
-    steps[0] = incoming[0, 0] + incoming[1, 0]
-    for t in range(1, total):
-        steps[t] = incoming[0, t] - incoming[0, t - 1] + incoming[1, t]
-    value = jnp.zeros_like(c)
-    for i in range(total):
-        value = (steps[start + stride * i] + value) * pivots[i]
-        steps[start + stride * i] = value
-    edge = jnp.where(right, 0.0, incoming[0, total - 1])
-    cut[0] = value - edge
-    swap = pltpu.make_async_remote_copy(
-        src_ref=cut.at[0], dst_ref=cut.at[1], send_sem=cut_sem.at[0], recv_sem=cut_sem.at[1],
-        device_id=mirror, device_id_type=MESH)
-    swap.start()
-    swap.wait_recv()
-    beyond = cut[1] - pivot * edge
-    value = (value + pivot * beyond) * inverse
-    phi[total] = jnp.where(right, 0.0, beyond + pivot * value)
-    phi[start + stride * (total - 1)] = value
-    for i in reversed(range(total - 1)):
-        value = steps[start + stride * i] + pivots[i] * value
-        phi[start + stride * i] = value
-
-    def homeward(peer, block):
+
+    def swap(k):
         return pltpu.make_async_remote_copy(
-            src_ref=phi.at[pl.ds(peer, 2)], dst_ref=home.at[block],
-            send_sem=back_send.at[peer], recv_sem=back_recv.at[block],
+            src_ref=cut.at[0, k], dst_ref=cut.at[1, k], send_sem=cut_sem.at[0, k],
+            recv_sem=cut_sem.at[1, k], device_id=mirror, device_id_type=MESH)
+
+    def homeward(k, peer, block):
+        return pltpu.make_async_remote_copy(
+            src_ref=phi.at[k, pl.ds(peer, 2)], dst_ref=home.at[k, block],
+            send_sem=back_send.at[k, peer], recv_sem=back_recv.at[k, block],
             device_id={"tm": base + peer}, device_id_type=MESH)
 
-    for peer in peers:
-        homeward(peer, me).start()
-    home[me, 0] = phi[me]
-    home[me, 1] = phi[me + 1]
-    for peer in peers:
-        homeward(peer, peer).wait_recv()
-
-    def final(k):
+    def relay(k, block):
         return pltpu.make_async_remote_copy(
-            src_ref=psend.at[k], dst_ref=precv.at[k], send_sem=fin_send.at[k],
-            recv_sem=fin_recv.at[k], device_id=other, device_id_type=MESH)
-
-    finals = [final(0), final(1)]
-    for k in range(2):
-        modes = home[:, k].reshape(rows, count)
-        part = by_table(modes, coli_v)
-        whole = table_by(rowi_v, part)
-        psend[k] = whole[:rows + 8]
-        finals[k].start()
-        pown[k] = whole[rows + 8:]
-    finals[0].wait_recv()
-    finals[1].wait_recv()
+            src_ref=home.at[k, block], dst_ref=across.at[k, block],
+            send_sem=fin_send.at[k, block], recv_sem=fin_recv.at[k, block],
+            device_id=other, device_id_type=MESH)
+
+    ends = []
+    for k in range(CHUNKS):
+        span = slice(k * part, (k + 1) * part)
+        for peer in reversed(peers):
+            arrival(0, k, peer).wait_recv()
+            arrival(1, k, peer).wait_recv()
+        steps[0, span] = incoming[0, 0, span] + incoming[1, 0, span]
+        for t in range(1, total):
+            steps[t, span] = (
+                incoming[0, t, span] - incoming[0, t - 1, span] + incoming[1, t, span])
+        value = jnp.zeros((part, count), jnp.float32)
+        for i in range(total):
+            value = (steps[start + stride * i, span] + value) * pivots[i, span]
+            steps[start + stride * i, span] = value
+        edge = jnp.where(right, 0.0, incoming[0, total - 1, span])
+        cut[0, k] = value - edge
+        swap(k).start()
+        ends.append((value, edge))
+    for k in range(CHUNKS):
+        span = slice(k * part, (k + 1) * part)
+        value, edge = ends[k]
+        swap(k).wait_recv()
+        pivot = pivots[total - 1, span]
+        beyond = cut[1, k] - pivot * edge
+        value = (value + pivot * beyond) * inverse[span]
+        phi[k, total] = jnp.where(right, 0.0, beyond + pivot * value)
+        phi[k, start + stride * (total - 1)] = value
+        for i in reversed(range(total - 1)):
+            value = steps[start + stride * i, span] + pivots[i, span] * value
+            phi[k, start + stride * i] = value
+        for peer in peers:
+            homeward(k, peer, me).start()
+        home[k, me, 0] = phi[k, me]
+        home[k, me, 1] = phi[k, me + 1]
+        relay(k, me).start()
+    for k in range(CHUNKS):
+        for peer in reversed(peers):
+            homeward(k, peer, peer).wait_recv()
+            relay(k, peer).start()
+    for k in range(CHUNKS):
+        for block in [me] + peers:
+            relay(k, block).wait_recv()
+
+    def modes(ref, field):
+        return jnp.concatenate(
+            [ref[k, block, field] for block in range(total) for k in range(CHUNKS)], axis=0)
+
+    for field in range(2):
+        both = jnp.concatenate([modes(home, field), modes(across, field)], axis=0)
+        fields[field] = by_table(table_by(rowi_v, both), coli_v)
     swap_rho.wait_send()
     swap_div.wait_send()
-    for peer in peers:
-        outward(0, peer).wait_send()
-        outward(1, peer).wait_send()
-        homeward(peer, me).wait_send()
-    for copy in finals:
-        copy.wait_send()
-    swap.wait_send()
-
-
-def finish_kernel(rho, mx, my, pown, precv, out_d, out_x, out_y, res_d, res_x, res_y, store_sem):
+    for k in range(CHUNKS):
+        swap(k).wait_send()
+        relay(k, me).wait_send()
+        for peer in peers:
+            outward(0, k, peer).wait_send()
+            outward(1, k, peer).wait_send()
+            homeward(k, peer, me).wait_send()
+            relay(k, peer).wait_send()
+
+
+def finish_kernel(rho, mx, my, fields, out_d, out_x, out_y, res_d, res_x, res_y, store_sem):
     rows, count = rho.shape
     col = lax.broadcasted_iota(jnp.int32, (rows, count), 1)
-    pot = pown[0] + precv[0]
+    pot = fields[0]
     here = pot[:rows]
     grad = pltpu.roll(pot, rows + 7, 0)[:rows] - here
     res_x[...] = mx[...] - flux_weight * grad
@@ -420,7 +442,7 @@
     res_y[...] = my[...] - flux_weight * grad
     save_y = pltpu.make_async_copy(res_y, out_y.at[0], store_sem.at[1])
     save_y.start()
-    res_d[...] = rho[...] - (here - (pown[1, :rows] + precv[1, :rows]))
+    res_d[...] = rho[...] - (here - fields[1, :rows])
     save_d = pltpu.make_async_copy(res_d, out_d.at[0], store_sem.at[2])
     save_d.start()
     for save in (save_x, save_y, save_d):
@@ -432,6 +454,7 @@
     parts = lax.axis_size("space")
     total = lax.axis_size("tm") // 2
     group = rows // total
+    part = group // CHUNKS
     tables = host_tables(count, parts, total)
     f32, bf16 = jnp.float32, jnp.bfloat16
     vm = pltpu.VMEM
@@ -439,15 +462,16 @@
     slab = vm((rows, count), f32)
     scratch = [slab] * 3 + [
         vm((2, count, count), bf16), vm((2, count, count), bf16),
-        vm((2, rows, count), bf16), vm((2, 2 * (rows + 8), rows), bf16),
+        vm((2, rows, count), bf16), vm((2, rows + 8, count), bf16),
         vm((rows, 128), f32), vm((group, count), f32),
         vm((rows + 8, count), f32), vm((2 * rows + 8, count), f32), vm((2 * rows + 8, count), f32),
         vm((2, total, group, count), f32), vm((2, total, group, count), f32),
-        vm((total, group, count), f32), vm((total + 1, group, count), f32),
-        vm((total, 2, group, count), f32),
-        vm((2, rows + 8, count), f32), vm((total, group, count), f32), vm((2, group, count), f32),
-        dma((9,)), dma((2,)), dma((2,)), dma((2, total)), dma((2, total)),
-        dma((total,)), dma((total,)), dma((2,)), dma((2,)), dma((2,)),
+        vm((total, group, count), f32), vm((CHUNKS, total + 1, part, count), f32),
+        vm((CHUNKS, total, 2, part, count), f32), vm((CHUNKS, total, 2, part, count), f32),
+        vm((total, group, count), f32), vm((2, CHUNKS, part, count), f32),
+        dma((9,)), dma((2,)), dma((2,)), dma((2, CHUNKS, total)), dma((2, CHUNKS, total)),
+        dma((CHUNKS, total)), dma((CHUNKS, total)), dma((CHUNKS, total)), dma((CHUNKS, total)),
+        dma((2, CHUNKS)),
     ]
     anywhere = pl.BlockSpec(memory_space=pl.ANY)
 
@@ -458,16 +482,16 @@
     pair = vm((2, rows + 8, count), f32)
     held = pl.pallas_call(
         kernel,
-        out_shape=[slab, slab, slab, pair, pair],
+        out_shape=[slab, slab, slab, pair],
         in_specs=[anywhere] * 9,
-        out_specs=[local] * 5,
+        out_specs=[local] * 4,
         scratch_shapes=scratch,
         compiler_params=pltpu.CompilerParams(collective_id=0, has_side_effects=True),
     )(density, flux_x, flux_y, *tables)
     return pl.pallas_call(
         finish_kernel,
         out_shape=[jax.ShapeDtypeStruct(density.shape, f32)] * 3,
-        in_specs=[local] * 5,
+        in_specs=[local] * 4,
         out_specs=[anywhere] * 3,
         scratch_shapes=[slab, slab, slab, dma((3,))],
     )(*[pltpu.with_memory_space_constraint(x, pltpu.VMEM) for x in held])
@@ -476,7 +500,7 @@
 def per_device(density, flux_x, flux_y):
     slabs, rows, count = density.shape
     size = lax.axis_size("tm")
-    fits = slabs == 1 and lax.axis_size("space") == 2 and size % 2 == 0 and rows % (4 * size) == 0
+    fits = slabs == 1 and lax.axis_size("space") == 2 and size % 2 == 0 and rows % (4 * CHUNKS * size) == 0
     return (per_device_kernel if fits and count % 128 == 0 else per_device_xla)(
         density, flux_x, flux_y)
 

time: 25.1 us -> 24.6 us (0.980)
  Pallas kernels: 24.3 us -> 23.8 us
    pallas_call x1, Pallas kernels: 23.4 us -> 23 us  [per_device_kernel(): pl.pallas_call(kernel, out_shape=[slab, slab, slab, pair], in_specs=[anyw...]
where the time goes in v4:
time: 24.6 us; the launch traced here: 24.5 us
  Pallas kernels  23.8 us (97%)
  between operations  0.64 us (3%)
    pallas_call x1, Pallas kernels, per_device_kernel(): pl.pallas_call(kernel, out_shape=[slab, slab, slab, pair], in_specs=[anyw...  23 us
    pallas_call x1, Pallas kernels, per_device_kernel(): pl.pallas_call(finish_kernel, out_shape=[jax.ShapeDtypeStruct(density.sha...  0.83 us

profile of v4, /device:TPU:1, one launch (start us, length us, event | category | flops | bytes accessed | tf_op | source)
XLA Modules:
  0.0 24.5 jit_solution(11763170727436292942)
XLA Ops:
  0.6 23.0 %shard_map.112 = (f32[128,256]{1,0:T(8,128)S(1)}, f32[128,256]{1,0:T(8,128)S(1)}, f32[128,256]{1,0:T(8,128)S(1)}, f32[2,136,256]{2,1,0:T(8,128)S(1)}) custom-call(f32[1,128,256]{2,1,0:T(8,128)} %refs_0_.1, f32[1,128,256]{2,1,0:T(8,128)} %refs_1_.1, f32[1,128,256]{2,1,0:T(8,128)} %refs_2_.1, bf16[2,256,256]{2,1,0:T(8,128)(2,1)} %constant.12.clone.refs_3_, ...), custom_call_target="tpu_custom_call" | custom-call | tf_op jit(solution)/shard_map/pallas_call | solution.py:483
  23.6 0.8 %shard_map.113 = (f32[1,128,256]{2,1,0:T(8,128)}, f32[1,128,256]{2,1,0:T(8,128)}, f32[1,128,256]{2,1,0:T(8,128)}) custom-call(f32[128,256]{1,0:T(8,128)S(1)} %get-tuple-element.7.rho, f32[128,256]{1,0:T(8,128)S(1)} %get-tuple-element.8.mx, f32[128,256]{1,0:T(8,128)S(1)} %get-tuple-element.9.my, f32[2,136,256]{2,1,0:T(8,128)S(1)} %get-tuple-element.10.fields), custom_call_target="tpu_custom_call" | custom-call | tf_op jit(solution)/shard_map/pallas_call | solution.py:491

commit v5 on v4

--- a/solution.py
+++ b/solution.py
@@ -259,8 +259,10 @@
     ]
     for load in loads:
         load.start()
-    near = sorted(range(1, total), key=lambda j: -min(j, total - j))
-    peers = [lax.rem(me + j, total) for j in near]
+    bits = [1 << i for i in range(total.bit_length() - 1)]
+    flips = [bit * (1 - 2 * lax.rem(me // bit, 2)) for bit in bits]
+    masks = sorted(range(1, total), key=lambda m: (-bin(m).count("1"), -m))
+    peers = [me + sum(f for f, bit in zip(flips, bits) if m & bit) for m in masks]
     other = {"space": 1 - side}
     barrier = pltpu.get_barrier_semaphore()
     for peer in peers:
@@ -500,7 +502,7 @@
 def per_device(density, flux_x, flux_y):
     slabs, rows, count = density.shape
     size = lax.axis_size("tm")
-    fits = slabs == 1 and lax.axis_size("space") == 2 and size % 2 == 0 and rows % (4 * CHUNKS * size) == 0
+    fits = slabs == 1 and lax.axis_size("space") == 2 and size % 2 == 0 and rows % (4 * CHUNKS * size) == 0 and size & (size - 1) == 0
     return (per_device_kernel if fits and count % 128 == 0 else per_device_xla)(
         density, flux_x, flux_y)
 

time: 24.6 us -> 23.4 us (0.951)
  Pallas kernels: 23.8 us -> 22.7 us
    pallas_call x1, Pallas kernels: 23 us -> 21.8 us  [per_device_kernel(): pl.pallas_call(kernel, out_shape=[slab, slab, slab, pair], in_specs=[anyw...]
where the time goes in v5:
time: 23.4 us; the launch traced here: 23.3 us
  Pallas kernels  22.7 us (97%)
  between operations  0.64 us (3%)
    pallas_call x1, Pallas kernels, per_device_kernel(): pl.pallas_call(kernel, out_shape=[slab, slab, slab, pair], in_specs=[anyw...  21.8 us
    pallas_call x1, Pallas kernels, per_device_kernel(): pl.pallas_call(finish_kernel, out_shape=[jax.ShapeDtypeStruct(density.sha...  0.83 us

profile of v5, /device:TPU:1, one launch (start us, length us, event | category | flops | bytes accessed | tf_op | source)
XLA Modules:
  0.0 23.3 jit_solution(13281807217698176274)
XLA Ops:
  0.6 21.8 %shard_map.112 = (f32[128,256]{1,0:T(8,128)S(1)}, f32[128,256]{1,0:T(8,128)S(1)}, f32[128,256]{1,0:T(8,128)S(1)}, f32[2,136,256]{2,1,0:T(8,128)S(1)}) custom-call(f32[1,128,256]{2,1,0:T(8,128)} %refs_0_.1, f32[1,128,256]{2,1,0:T(8,128)} %refs_1_.1, f32[1,128,256]{2,1,0:T(8,128)} %refs_2_.1, bf16[2,256,256]{2,1,0:T(8,128)(2,1)} %constant.12.clone.refs_3_, ...), custom_call_target="tpu_custom_call" | custom-call | tf_op jit(solution)/shard_map/pallas_call | solution.py:485
  22.5 0.8 %shard_map.113 = (f32[1,128,256]{2,1,0:T(8,128)}, f32[1,128,256]{2,1,0:T(8,128)}, f32[1,128,256]{2,1,0:T(8,128)}) custom-call(f32[128,256]{1,0:T(8,128)S(1)} %get-tuple-element.7.rho, f32[128,256]{1,0:T(8,128)S(1)} %get-tuple-element.8.mx, f32[128,256]{1,0:T(8,128)S(1)} %get-tuple-element.9.my, f32[2,136,256]{2,1,0:T(8,128)S(1)} %get-tuple-element.10.fields), custom_call_target="tpu_custom_call" | custom-call | tf_op jit(solution)/shard_map/pallas_call | solution.py:493
